TPU v7x, 256 devices: a whole 4x4x8 slice. The times are simulated.
256 devices in a mesh: space: 32 (over y, z_hi, core), test: 2 (over z_lo), trial: 4 (over x).
Axes of the slice: x: 4, y: 4, z: 8 (z_hi: 4, z_lo: 2; z = z_hi * 2 + z_lo), core: 2. Of those that a mesh axis runs over, the one named last changes fastest.
Arguments:
- test_modes: bfloat16 [3, 128, 128, 8, 128], P(None, 'test', 'space'), may hold values from -6 to 6
- trial_modes: bfloat16 [3, 128, 128, 8, 128], P(None, 'trial', 'space'), may hold values from -6 to 6
- volumes: float32 [128, 8, 128], P('space'), may hold values from 0.25 to 4
Outputs:
- tensor: float32 [128, 128, 128], P('space', 'test', 'trial')
All inputs are finite; a program needn't handle non-finite values.
Results may differ from a plain program's by a relative error of at most 0.0051.
Values may be sent and summed in bfloat16 or wider, within the bound.
No kernel may reach another device: no remote copies, remote signals or barrier semaphores. Data moves between devices by JAX's collectives and lax.ppermute only.
A program may use at most 64 MiB of HBM per device.

v0:
```python
import math
import jax
import jax.numpy as jnp
from jax import lax
from jax.sharding import PartitionSpec as P


def with_halo(cells, sides, width):
    for axis, dim in sides:
        count = lax.axis_size(axis)
        ends = count - 1
        head = lax.slice_in_dim(cells, 0, width, axis=dim)
        tail = lax.slice_in_dim(cells, cells.shape[dim] - width, cells.shape[dim], axis=dim)
        cells = jnp.concatenate(
            [
                lax.ppermute(tail, axis, [(i, (i + 1) % count) for i in range(ends)]),
                cells,
                lax.ppermute(head, axis, [((i + 1) % count, i) for i in range(ends)]),
            ],
            axis=dim,
        )
    return cells


def derivatives(padded):
    field = padded.astype(jnp.float32)
    along_x = (field[:, :, 2:] - field[:, :, :-2]) * 0.5
    center = field[:, :, 1:-1]
    wide_y = jnp.pad(center, ((0, 0), (0, 0), (0, 0), (1, 1), (0, 0)))
    along_y = (wide_y[:, :, :, 2:] - wide_y[:, :, :, :-2]) * 0.5
    wide_z = jnp.pad(center, ((0, 0), (0, 0), (0, 0), (0, 0), (1, 1)))
    along_z = (wide_z[:, :, :, :, 2:] - wide_z[:, :, :, :, :-2]) * 0.5
    return jnp.stack([along_x, along_y, along_z], axis=1).astype(jnp.bfloat16)


def pick_row(array, plane, row, first):
    return lax.dynamic_index_in_dim(
        lax.dynamic_index_in_dim(array, plane, first, False), row, first, False
    )


def block_terms(mode_rows, grad_rows, weighted):
    width_j = mode_rows.shape[1]
    width_k = grad_rows.shape[2]
    planes = mode_rows.shape[2]
    rows_each = mode_rows.shape[3]

    def advance(position, running):
        plane = position // rows_each
        row = position % rows_each
        trial_block = pick_row(mode_rows, plane, row, 2)
        grad_block = pick_row(grad_rows, plane, row, 3)
        test_block = pick_row(weighted, plane, row, 2)
        convected = jnp.einsum(
            "bjc,abkc->ajkc", trial_block, grad_block, preferred_element_type=jnp.float32
        ).astype(jnp.bfloat16)
        return running + jnp.einsum(
            "aic,ajkc->jik", test_block, convected, preferred_element_type=jnp.float32
        )

    running = jnp.zeros((width_j, weighted.shape[1], width_k), jnp.float32)
    return lax.fori_loop(0, planes * rows_each, advance, running)


def finish(partial_value, factor):
    return lax.psum_scatter(partial_value, "space", scatter_dimension=0, tiled=True) * factor


def shards(test_modes, trial_modes, volumes):
    cell_count = trial_modes.shape[2] * trial_modes.shape[3] * trial_modes.shape[4]
    factor = 1.0 / (4.0 * math.sqrt(cell_count * lax.axis_size("space")))
    padded = with_halo(trial_modes, (("space", 2),), 1)
    gradients = derivatives(padded)
    weighted = (test_modes.astype(jnp.float32) * volumes).astype(jnp.bfloat16)
    all_modes = lax.all_gather(trial_modes, "trial", axis=1, tiled=True)
    partial_value = block_terms(all_modes, gradients, weighted)
    return finish(partial_value, factor)


def solution(mesh):
    return jax.shard_map(
        shards,
        mesh=mesh,
        in_specs=(
            P(None, "test", "space", None, None),
            P(None, "trial", "space", None, None),
            P("space", None, None),
        ),
        out_specs=P("space", "test", "trial"),
        check_vma=False,
    )
```

profile of v0, /device:TPU:2, one launch (start us, length us, event | category | flops | bytes accessed | tf_op | source)
XLA Modules:
  0.0 535.8 jit_solution(14520357436832206297)
XLA Ops:
  21.6 31.8 %all-gather.2.cloned.1.call-done = bf16[3,128,4,8,128]{4,1,0,3,2:T(8,128)(2,1)} async-done(((bf16[3,32,4,8,128]{4,1,0,3,2:T(8,128)(2,1)}), bf16[3,128,4,8,128]{4,1,0,3,2:T(8,128)(2,1)}) %all-gather.2.cloned.1.call-update) | async-done | bytes 3145744 | tf_op jit(solution)/shard_map/all_gather | solution.py:75
  53.4 376.8 %while.17 = (s32[]{:T(128)}, f32[128,64,32]{0,1,2:T(8,128)}, bf16[3,3,32,4,8,128]{5,2,1,0,4,3:T(8,128)(2,1)}, bf16[3,128,4,8,128]{4,1,0,3,2:T(8,128)(2,1)}, bf16...) while((s32[]{:T(128)}, f32[128,64,32]{0,1,2:T(8,128)}, ...), condition=%wide.region_1.2_spmd.clone, body=%wide.region_0.1_spmd.clone.sunk | while | flops 211288080 | bytes 15589742 | solution.py:62
  58.0 3.8 copy.26
  81.1 3.8 copy.26
  92.9 3.8 copy.26
  104.7 3.8 copy.26
  116.5 3.8 copy.26
  128.3 3.8 copy.26
  140.1 3.8 copy.26
  151.9 3.8 copy.26
  163.7 3.8 copy.26
  175.5 3.8 copy.26
  187.3 3.8 copy.26
  199.0 3.8 copy.26
  210.8 3.8 copy.26
  222.6 3.8 copy.26
  234.4 3.8 copy.26
  246.2 3.8 copy.26
  269.8 3.8 copy.26
  281.6 3.8 copy.26
  305.1 3.8 copy.26
  316.9 3.8 copy.26
  328.7 3.8 copy.26
  340.5 3.8 copy.26
  352.3 3.8 copy.26
  364.1 3.8 copy.26
  375.9 3.8 copy.26
  387.7 3.8 copy.26
  399.5 3.8 copy.26
  411.3 3.8 copy.26
  430.2 4.0 copy.15
  434.2 93.2 %reduce-scatter.2.cloned.1.call-done = f32[4,64,32]{1,2,0:T(8,128)} async-done(((f32[128,64,32]{1,2,0:T(8,128)}), f32[4,64,32]{1,2,0:T(8,128)}) %reduce-scatter.2.cloned.1.call-update) | async-done | bytes 32784 | tf_op jit(solution)/shard_map/reduce_scatter | solution.py:66
  (219 shorter events, 286.4 us)
Async XLA Ops:
  6.5 6.7 %copy-start.1 = (bf16[3,64,4,8,128]{4,3,2,1,0:T(8,128)(2,1)S(1)}, bf16[3,64,4,8,128]{4,3,2,1,0:T(8,128)(2,1)}, u32[]{:S(2)}) copy-start(bf16[3,64,4,8,128]{4,3,2,1,0:T(8,128)(2,1)} %param.5) | copy-start | bytes 4718596
  6.5 6.7 %copy-start.2 = (f32[4,8,128]{2,1,0:T(8,128)S(1)}, f32[4,8,128]{2,1,0:T(8,128)}, u32[]{:S(2)}) copy-start(f32[4,8,128]{2,1,0:T(8,128)} %param.7) | copy-start | bytes 49156
  6.5 46.8 %all-gather.2.cloned.1.call-start = ((), (), s32[]{:S(2)}) async-start(), calls=%async_computation.1 | async-start | bytes 3932160 | tf_op jit(solution)/shard_map/all_gather | solution.py:75
  9.0 518.5 %reduce-scatter.2.cloned.1.call-start = ((), (), s32[]{:S(2)}) async-start(), calls=%async_computation.2 | async-start | bytes 2162688 | tf_op jit(solution)/shard_map/reduce_scatter | solution.py:66
  10.1 5.0 collective-permute-start
  11.9 6.4 %collective-permute-start.1 = (bf16[3,32,1,8,128]{4,1,0,3,2:T(8,128)(2,1)S(1)}, bf16[3,32,1,8,128]{4,1,0,3,2:T(8,128)(2,1)S(1)}, u32[]{:S(2)}, u32[]{:S(2)}) collective-permute-start(bf16[3,32,1,8,128]{4,1,0,3,2:T(8,128)(2,1)S(1)} %get-tuple-element.203), channel_id=1, source_target_pairs={{8,0},{16,8},{24,16},{32,24},{40,32},{48,40},{56,48},{64,56},{72,6... | collective-permute-start | bytes 589832 | tf_op jit(solution)/shard_map/ppermute | solution.py:18
  13.2 5.1 copy-start
Sparse Core Ops, SparseCore 0:
  9.1 44.1 all-gather.1
  434.4 93.0 reduce-scatter.1
where the time goes:
time: 541 us; the launch traced here: 536 us
  local copies, waits for them, and re-layouts  198 us (37%)
  matrix products  186 us (34%)
  waiting for transfers between devices  128 us (24%)
  between operations  13.5 us (2%)
  other arithmetic  6.63 us (1%)
    dot_general x32, local copies, waits for them, and re-layouts, advance(): jnp.einsum('bjc,abkc->ajkc', trial_block, grad_block, preferred_element_t...  121 us
    dot_general x32, matrix products, advance(): jnp.einsum('aic,ajkc->jik', test_block, convected, preferred_element_type...  106 us
    reduce_scatter x1, waiting for transfers between devices, finish(): lax.psum_scatter(partial_value, 'space', scatter_dimension=0, tiled=True)  93.2 us
    dot_general x32, matrix products, advance(): jnp.einsum('bjc,abkc->ajkc', trial_block, grad_block, preferred_element_t...  79.3 us
    squeeze x128, local copies, waits for them, and re-layouts, pick_row(): lax.dynamic_index_in_dim(lax.dynamic_index_in_dim(array, plane, first, Fa...  69.2 us
    all_gather x1, waiting for transfers between devices, shards(): all_modes = lax.all_gather(trial_modes, 'trial', axis=1, tiled=True)  31.8 us
  transfers between devices with their start and end apart: 4, of which 3 were waited for; matrix products, arithmetic and copies ran while one was open for 1% of the time, Pallas kernels for 0%

commit v1 on v0

--- a/solution.py
+++ b/solution.py
@@ -72,7 +72,10 @@
     padded = with_halo(trial_modes, (("space", 2),), 1)
     gradients = derivatives(padded)
     weighted = (test_modes.astype(jnp.float32) * volumes).astype(jnp.bfloat16)
-    all_modes = lax.all_gather(trial_modes, "trial", axis=1, tiled=True)
+    size = lax.axis_size("trial")
+    blocks = jnp.stack([trial_modes for _ in range(size)])
+    blocks = lax.all_to_all(blocks, "trial", split_axis=0, concat_axis=0)
+    all_modes = jnp.concatenate(blocks, axis=1)
     partial_value = block_terms(all_modes, gradients, weighted)
     return finish(partial_value, factor)
 

time: 541 us -> 371 us (0.69)
  local copies, waits for them, and re-layouts: 198 us -> 100 us
  matrix products: 186 us -> 116 us
  waiting for transfers between devices: 128 us -> 120 us
  starting transfers between devices: 3.09 us -> 10.2 us
    dot_general x32 -> x0, local copies, waits for them, and re-layouts: 121 us -> none  [advance(): jnp.einsum('bjc,abkc->ajkc', trial_block, grad_block, preferred_element_t...]
    while x0 -> x128, local copies, waits for them, and re-layouts: none -> 46.3 us
    dot_general x32, matrix products: 79.3 us -> 42.3 us  [advance(): jnp.einsum('bjc,abkc->ajkc', trial_block, grad_block, preferred_element_t...]
    dot_general x32, matrix products: 106 us -> 73.7 us  [advance(): jnp.einsum('aic,ajkc->jik', test_block, convected, preferred_element_type...]
    all_gather x1 -> x0, waiting for transfers between devices: 31.8 us -> none  [shards(): all_modes = lax.all_gather(trial_modes, 'trial', axis=1, tiled=True)]
    squeeze x128, local copies, waits for them, and re-layouts: 69.2 us -> 40.6 us  [pick_row(): lax.dynamic_index_in_dim(lax.dynamic_index_in_dim(array, plane, first, Fa...]
    all_to_all x0 -> x1, waiting for transfers between devices: none -> 24.2 us  [shards(): blocks = lax.all_to_all(blocks, 'trial', split_axis=0, concat_axis=0)]
    all_to_all x0 -> x1, starting transfers between devices: none -> 6.97 us  [shards(): blocks = lax.all_to_all(blocks, 'trial', split_axis=0, concat_axis=0)]
where the time goes in v1:
time: 371 us; the launch traced here: 369 us
  waiting for transfers between devices  120 us (32%)
  matrix products  116 us (31%)
  local copies, waits for them, and re-layouts  100 us (27%)
  between operations  13.5 us (4%)
  starting transfers between devices  10.2 us (3%)
  other arithmetic  6.09 us (2%)
    reduce_scatter x1, waiting for transfers between devices, finish(): lax.psum_scatter(partial_value, 'space', scatter_dimension=0, tiled=True)  94.5 us
    dot_general x32, matrix products, advance(): jnp.einsum('aic,ajkc->jik', test_block, convected, preferred_element_type...  73.7 us
    while x128, local copies, waits for them, and re-layouts  46.3 us
    dot_general x32, matrix products, advance(): jnp.einsum('bjc,abkc->ajkc', trial_block, grad_block, preferred_element_t...  42.3 us
    squeeze x128, local copies, waits for them, and re-layouts, pick_row(): lax.dynamic_index_in_dim(lax.dynamic_index_in_dim(array, plane, first, Fa...  40.6 us
    all_to_all x1, waiting for transfers between devices, shards(): blocks = lax.all_to_all(blocks, 'trial', split_axis=0, concat_axis=0)  24.2 us
  transfers between devices with their start and end apart: 4, of which 3 were waited for; matrix products, arithmetic and copies ran while one was open for 1% of the time, Pallas kernels for 0%

profile of v1, /device:TPU:2, one launch (start us, length us, event | category | flops | bytes accessed | tf_op | source)
XLA Modules:
  0.0 369.3 jit_solution(12668376838836254584)
XLA Ops:
  8.0 2.3 stack.27
  10.3 7.0 %all-to-all-start = ((bf16[4,3,32,4,8,128]{5,2,1,4,3,0:T(8,128)(2,1)}), bf16[4,3,32,4,8,128]{5,2,1,4,3,0:T(8,128)(2,1)}, u32[]{:S(2)}, u32[]{:S(2)}) async-start(bf16[4,3,32,4,8,128]{5,2,1,4,3,0:T(8,128)(2,1)} %stack.27), calls=%async_computation | async-start | bytes 6291456 | tf_op jit(solution)/shard_map/all_to_all | solution.py:77
  27.7 24.2 %all-to-all-done = bf16[4,3,32,4,8,128]{5,2,1,4,3,0:T(8,128)(2,1)} async-done(((bf16[4,3,32,4,8,128]{5,2,1,4,3,0:T(8,128)(2,1)}), bf16[4,3,32,4,8,128]{5,2,1,4,3,0:T(8,128)(2,1)}, u32[]{:S(2)}, u32[]{:S(2)}) %all-to-all-start) | async-done | bytes 3145760 | tf_op jit(solution)/shard_map/all_to_all | solution.py:77
  51.9 3.1 copy.36
  55.0 2.8 copy.38
  57.8 205.9 %while.17 = (s32[]{:T(128)}, f32[128,64,32]{0,1,2:T(8,128)S(1)}, bf16[3,3,32,4,8,128]{5,2,1,0,4,3:T(8,128)(2,1)S(1)}, bf16[3,128,4,8,128]{4,1,0,3,2:T(8,128)(2,1...) while((s32[]{:T(128)}, f32[128,64,32]{0,1,2:T(8,128)S(1)}, ...), condition=%wide.region_1.2_spmd.clone, body=%wide.region_0.1_spmd.clone.sunk | while | flops 212860944 | bytes 28172716 | solution.py:62
  61.9 2.3 fusion.34
  68.4 2.3 fusion.34
  74.8 2.3 fusion.34
  81.2 2.3 fusion.34
  87.7 2.3 fusion.34
  94.1 2.3 fusion.34
  107.0 2.3 fusion.34
  113.4 2.3 fusion.34
  119.8 2.3 fusion.34
  132.7 2.3 fusion.34
  152.0 2.3 fusion.34
  158.4 2.3 fusion.34
  164.9 2.3 fusion.34
  171.3 2.3 fusion.34
  177.7 2.3 fusion.34
  190.6 2.3 fusion.34
  203.5 2.3 fusion.34
  209.9 2.3 fusion.34
  216.3 2.3 fusion.34
  222.8 2.3 fusion.34
  229.2 2.3 fusion.34
  235.6 2.3 fusion.34
  248.5 2.3 fusion.34
  261.4 2.3 fusion.34
  263.7 2.8 copy.39
  266.5 94.5 %reduce-scatter.2.cloned.1.call-done = f32[4,64,32]{1,2,0:T(8,128)} async-done(((f32[128,64,32]{1,2,0:T(8,128)}), f32[4,64,32]{1,2,0:T(8,128)}) %reduce-scatter.2.cloned.1.call-update) | async-done | bytes 32784 | tf_op jit(solution)/shard_map/reduce_scatter | solution.py:66
  (315 shorter events, 160.9 us)
Async XLA Ops:
  10.3 11.1 %copy-start.2 = (bf16[3,64,4,8,128]{4,3,2,1,0:T(8,128)(2,1)S(1)}, bf16[3,64,4,8,128]{4,3,2,1,0:T(8,128)(2,1)}, u32[]{:S(2)}) copy-start(bf16[3,64,4,8,128]{4,3,2,1,0:T(8,128)(2,1)} %param.5) | copy-start | bytes 4718596
  10.3 11.1 %copy-start.3 = (f32[4,8,128]{2,1,0:T(8,128)S(1)}, f32[4,8,128]{2,1,0:T(8,128)}, u32[]{:S(2)}) copy-start(f32[4,8,128]{2,1,0:T(8,128)} %param.7) | copy-start | bytes 49156
  10.3 41.6 %all-to-all-start = ((bf16[4,3,32,4,8,128]{5,2,1,4,3,0:T(8,128)(2,1)}), bf16[4,3,32,4,8,128]{5,2,1,4,3,0:T(8,128)(2,1)}, u32[]{:S(2)}, u32[]{:S(2)}) async-start(bf16[4,3,32,4,8,128]{5,2,1,4,3,0:T(8,128)(2,1)} %stack.27), calls=%async_computation | async-start | bytes 6291456 | tf_op jit(solution)/shard_map/all_to_all | solution.py:77
  17.3 343.7 %reduce-scatter.2.cloned.1.call-start = ((), (), s32[]{:S(2)}) async-start(), calls=%async_computation.2 | async-start | bytes 2162688 | tf_op jit(solution)/shard_map/reduce_scatter | solution.py:66
  18.1 5.1 %collective-permute-start = (bf16[3,32,1,8,128]{4,1,0,3,2:T(8,128)(2,1)}, bf16[3,32,1,8,128]{4,1,0,3,2:T(8,128)(2,1)}, u32[]{:S(2)}, u32[]{:S(2)}) collective-permute-start(bf16[3,32,1,8,128]{4,1,0,3,2:T(8,128)(2,1)} %get-tuple-element.207), channel_id=1, source_target_pairs={{0,8},{8,16},{16,24},{24,32},{32,40},{40,48},{48,56},{56,64},{64,7... | collective-permute-start | bytes 589832 | tf_op jit(solution)/shard_map/ppermute | solution.py:16
  20.0 4.8 %collective-permute-start.1 = (bf16[3,32,1,8,128]{4,1,0,3,2:T(8,128)(2,1)}, bf16[3,32,1,8,128]{4,1,0,3,2:T(8,128)(2,1)}, u32[]{:S(2)}, u32[]{:S(2)}) collective-permute-start(bf16[3,32,1,8,128]{4,1,0,3,2:T(8,128)(2,1)} %get-tuple-element.208), channel_id=1, source_target_pairs={{8,0},{16,8},{24,16},{32,24},{40,32},{48,40},{56,48},{64,56},{72,6... | collective-permute-start | bytes 589832 | tf_op jit(solution)/shard_map/ppermute | solution.py:18
  61.9 2.3 copy-start.1
  68.3 2.3 copy-start.1
  74.8 2.3 copy-start.1
  81.2 2.3 copy-start.1
  87.6 2.3 copy-start.1
  94.1 2.3 copy-start.1
  100.5 2.3 copy-start.1
  106.9 2.3 copy-start.1
  113.4 2.3 copy-start.1
  119.8 2.3 copy-start.1
  126.2 2.3 copy-start.1
  132.7 2.3 copy-start.1
  152.0 2.3 copy-start.1
  158.4 2.3 copy-start.1
  164.9 2.3 copy-start.1
  171.3 2.3 copy-start.1
  177.7 2.3 copy-start.1
  190.6 2.3 copy-start.1
  203.5 2.3 copy-start.1
  209.9 2.3 copy-start.1
  216.3 2.3 copy-start.1
  222.8 2.3 copy-start.1
  229.2 2.3 copy-start.1
  235.6 2.3 copy-start.1
  248.5 2.3 copy-start.1
  261.4 2.3 copy-start.1
  (38 other events, 61.0 us)
Sparse Core Ops, SparseCore 0:
  266.7 94.2 reduce-scatter.1
